TPU v7x, 32 devices: a whole 2x2x4 slice. The times are simulated.
32 devices in a mesh: row: 8 (over z, x), col: 4 (over y, core).
Axes of the slice: x: 2, y: 2, z: 4, core: 2. Of those that a mesh axis runs over, the one named last changes fastest.
Arguments:
- tokens: bfloat16 [512, 8192], P('col', 'row'), may hold values from -6 to 6
- gate_weight: bfloat16 [8192, 14336], P('row', 'col'), may hold values from -0.09375 to 0.09375
- up_weight: bfloat16 [8192, 14336], P('row', 'col'), may hold values from -0.09375 to 0.09375
- down_weight: bfloat16 [14336, 8192], P('col', 'row'), may hold values from -0.09375 to 0.09375
- gate_mask: int32 [128, 224], P('row', 'col'), may hold values from 0 to 1, as said below
- up_mask: int32 [128, 224], P('row', 'col'), may hold values from 0 to 1, as said below
- down_mask: int32 [224, 128], P('col', 'row'), may hold values from 0 to 1, as said below
- head_weight: bfloat16 [8192, 128], P('row'), may hold values from -0.15625 to 0.15625
- labels: int32 [512], P('col'), may hold values from 0 to 127
Outputs:
- token_loss: float32 [512], P('col')
- tokens_grad: bfloat16 [512, 8192], P('col', 'row')
- gate_grad: bfloat16 [8192, 14336], P('row', 'col')
- up_grad: bfloat16 [8192, 14336], P('row', 'col')
- down_grad: bfloat16 [14336, 8192], P('col', 'row')
Inputs may be any that keep to these rules, and one draw needn't show every extreme that they name: `gate_mask`: 1 keeps a block of 64 x 64 weights, 0 prunes it. `up_mask`: 1 keeps a block of 64 x 64 weights, 0 prunes it. `down_mask`: 1 keeps a block of 64 x 64 weights, 0 prunes it.
All inputs are finite; a program needn't handle non-finite values.
Results may differ from a plain program's by a relative error of at most 0.011.
Values may be sent and summed in bfloat16 or wider, within the bound.
A program may use at most 192 MiB of HBM per device.

v0:
```python
import jax
import jax.numpy as jnp
from jax import lax
from jax.sharding import PartitionSpec as P

loss_scale = 8.0


def masked(weight, block_mask):
    height, breadth = weight.shape
    blocks = weight.reshape(
        block_mask.shape[0],
        height // block_mask.shape[0],
        block_mask.shape[1],
        breadth // block_mask.shape[1],
    )
    pruned = blocks * block_mask[:, None, :, None].astype(weight.dtype)
    return pruned.reshape(height, breadth)


def classify(logits, labels):
    exponent = jnp.exp(logits)
    partition = jnp.sum(exponent, axis=1, keepdims=True)
    classes = lax.broadcasted_iota(jnp.int32, logits.shape, 1)
    onehot = (labels[:, None] == classes).astype(jnp.float32)
    token_cost = jnp.log(partition[:, 0]) - jnp.sum(logits * onehot, axis=1)
    return (token_cost, loss_scale * (exponent / partition - onehot))


def token_product(panel_rows, weight, weight_axis):
    panel_axis = 0
    return lax.dot_general(
        panel_rows,
        weight,
        (((panel_axis,), (weight_axis,)), ((), ())),
        preferred_element_type=jnp.float32,
    )


def shards(
    tokens, gate_weight, up_weight, down_weight, gate_mask, up_mask, down_mask, head_weight, labels
):
    gate_kept = masked(gate_weight, gate_mask)
    up_kept = masked(up_weight, up_mask)
    down_kept = masked(down_weight, down_mask)
    every_token = lax.all_gather(tokens, "col", axis=0, tiled=True)
    gate_part = lax.dot_general(
        gate_kept, every_token, (((0,), (1,)), ((), ())), preferred_element_type=jnp.float32
    )
    up_part = lax.dot_general(
        up_kept, every_token, (((0,), (1,)), ((), ())), preferred_element_type=jnp.float32
    )
    stacked = lax.psum_scatter(
        jnp.concatenate([gate_part, up_part], axis=1), "row", scatter_dimension=0, tiled=True
    )
    midpoint = stacked.shape[1] // 2
    gate_sum = stacked[:, :midpoint]
    up_sum = stacked[:, midpoint:]
    sigmoid_gate = jax.nn.sigmoid(gate_sum)
    activated = gate_sum * sigmoid_gate
    hidden = (activated * up_sum).astype(jnp.bfloat16)
    hidden_all = lax.all_gather(hidden, "row", axis=0, tiled=True)
    branch = lax.psum_scatter(
        token_product(hidden_all, down_kept, 0), "col", scatter_dimension=0, tiled=True
    )
    mixed_rows = (tokens.astype(jnp.float32) + branch).astype(jnp.bfloat16)
    partial_value = jnp.dot(mixed_rows, head_weight, preferred_element_type=jnp.float32)
    logits = lax.psum(partial_value, "row")
    token_loss, grad_full = classify(logits, labels)
    dlogits = grad_full.astype(jnp.bfloat16)
    dmixed = lax.dot_general(
        dlogits, head_weight, (((1,), (1,)), ((), ())), preferred_element_type=jnp.float32
    ).astype(jnp.bfloat16)
    dmixed_all = lax.all_gather(dmixed, "col", axis=0, tiled=True)
    dhidden = lax.psum_scatter(
        lax.dot_general(
            down_kept, dmixed_all, (((1,), (1,)), ((), ())), preferred_element_type=jnp.float32
        ),
        "row",
        scatter_dimension=0,
        tiled=True,
    )
    gate_delta = (dhidden * up_sum * sigmoid_gate * (1.0 + gate_sum * (1.0 - sigmoid_gate))).astype(
        jnp.bfloat16
    )
    up_delta = (dhidden * activated).astype(jnp.bfloat16)
    gate_all, up_all = (
        lax.all_gather(gate_delta, "row", axis=0, tiled=True),
        lax.all_gather(up_delta, "row", axis=0, tiled=True),
    )
    token_axis = 1
    down_grad = masked(
        lax.dot_general(
            hidden_all,
            dmixed_all,
            (((token_axis,), (0,)), ((), ())),
            preferred_element_type=jnp.float32,
        ),
        down_mask,
    ).astype(jnp.bfloat16)
    gate_grad = masked(
        lax.dot_general(
            every_token,
            gate_all,
            (((0,), (token_axis,)), ((), ())),
            preferred_element_type=jnp.float32,
        ),
        gate_mask,
    ).astype(jnp.bfloat16)
    up_grad = masked(
        lax.dot_general(
            every_token,
            up_all,
            (((0,), (token_axis,)), ((), ())),
            preferred_element_type=jnp.float32,
        ),
        up_mask,
    ).astype(jnp.bfloat16)
    gate_term = token_product(gate_all, gate_kept, 1)
    up_term = token_product(up_all, up_kept, 1)
    input_sum = lax.psum_scatter(gate_term + up_term, "col", scatter_dimension=0, tiled=True)
    tokens_grad = (dmixed.astype(jnp.float32) + input_sum).astype(jnp.bfloat16)
    return (token_loss, tokens_grad, gate_grad, up_grad, down_grad)


def solution(mesh):
    placed = (
        P("col", "row"),
        P("row", "col"),
        P("row", "col"),
        P("col", "row"),
        P("row", "col"),
        P("row", "col"),
        P("col", "row"),
        P("row", None),
        P("col"),
    )
    return jax.shard_map(
        shards,
        mesh=mesh,
        in_specs=placed,
        out_specs=(P("col"), P("col", "row"), P("row", "col"), P("row", "col"), P("col", "row")),
        check_vma=False,
    )
```

profile of v0, /device:TPU:0, one launch (start us, length us, event | category | flops | bytes accessed | tf_op | source)
XLA Modules:
  0.0 1011.9 jit_solution(17688586089172399964)
XLA Ops:
  7.2 0.7 all-gather.6.cloned.1.call-update
  8.0 0.8 fusion.9
  8.7 7.2 mul.99
  15.9 18.9 %mul.100 = bf16[1024,3584]{1,0:T(8,128)(2,1)} reshape(bf16[16,64,56,64]{3,2,1,0:T(8,128)(2,1)} %mul.99) | data formatting | bytes 14680064 | tf_op jit(solution)/shard_map/mul | solution.py:17
  34.9 7.2 mul.96
  42.0 18.7 %mul.97 = bf16[1024,3584]{1,0:T(8,128)(2,1)} reshape(bf16[16,64,56,64]{3,2,1,0:T(8,128)(2,1)} %mul.96) | data formatting | bytes 14680064 | tf_op jit(solution)/shard_map/mul | solution.py:17
  60.8 10.2 %mul.101 = bf16[1024,3584]{1,0:T(8,128)(2,1)} multiply(bf16[1024,3584]{1,0:T(8,128)(2,1)} %param.11, bf16[1024,3584]{1,0:T(8,128)(2,1)} %mul.100) | non-fusion elementwise | flops 3670016 | bytes 22020096 | tf_op jit(solution)/shard_map/mul | solution.py:17
  71.0 10.2 %mul.98 = bf16[1024,3584]{1,0:T(8,128)(2,1)} multiply(bf16[1024,3584]{1,0:T(8,128)(2,1)} %param.10, bf16[1024,3584]{1,0:T(8,128)(2,1)} %mul.97) | non-fusion elementwise | flops 3670016 | bytes 22020096 | tf_op jit(solution)/shard_map/mul | solution.py:17
  81.2 6.6 fusion.15
  87.8 4.0 fusion.14
  91.8 5.5 pad_maximum_fusion
  97.3 15.7 %copy.43 = f32[3584,1024]{1,0:T(8,128)} copy(f32[3584,1024]{0,1:T(8,128)} %pad_maximum_fusion) | data formatting | bytes 29360128
  113.1 239.5 %reduce-scatter.13.cloned.1.call-done = f32[448,1024]{1,0:T(8,128)} async-done(((f32[3584,1024]{1,0:T(8,128)}), f32[448,1024]{1,0:T(8,128)}) %reduce-scatter.13.cloned.1.call-update) | async-done | bytes 1835024 | tf_op jit(solution)/shard_map/reduce_scatter | solution.py:53
  352.6 2.5 multiply_convert_fusion.3
  355.2 0.1 copy.33
  355.3 7.2 mul.104
  362.5 20.1 %mul.105 = bf16[3584,1024]{1,0:T(8,128)(2,1)} reshape(bf16[56,64,16,64]{3,2,1,0:T(8,128)(2,1)} %mul.104) | data formatting | bytes 14680064 | tf_op jit(solution)/shard_map/mul | solution.py:17
  382.6 12.5 %mul.106 = bf16[3584,1024]{1,0:T(8,128)(2,1)} multiply(bf16[3584,1024]{1,0:T(8,128)(2,1)} %param.12, bf16[3584,1024]{1,0:T(8,128)(2,1)} %mul.105) | non-fusion elementwise | flops 3670016 | bytes 22020096 | tf_op jit(solution)/shard_map/mul | solution.py:17
  395.1 25.5 %all-gather.8.cloned.1.call-done = bf16[3584,512]{1,0:T(8,128)(2,1)} async-done(((bf16[448,512]{1,0:T(8,128)(2,1)}), bf16[3584,512]{1,0:T(8,128)(2,1)}) %all-gather.8.cloned.1.call-update) | async-done | bytes 3670032 | tf_op jit(solution)/shard_map/all_gather | solution.py:62
  420.6 9.5 fusion.11
  430.2 30.0 %reduce-scatter.9.cloned.1.call-done = f32[128,1024]{1,0:T(8,128)} async-done(((f32[512,1024]{1,0:T(8,128)}), f32[128,1024]{1,0:T(8,128)}) %reduce-scatter.9.cloned.1.call-update) | async-done | bytes 524304 | tf_op jit(solution)/shard_map/reduce_scatter | solution.py:63
  460.2 1.9 fusion.3
  462.1 71.2 %all-reduce.2.cloned.1.call-done = f32[128,128]{1,0:T(8,128)} async-done(((f32[128,128]{1,0:T(8,128)}), f32[128,128]{1,0:T(8,128)}) %all-reduce.2.cloned.1.call-update) | async-done | bytes 65552 | tf_op jit(solution)/shard_map/psum | solution.py:68
  533.3 1.0 exponential_reduce_fusion
  534.3 1.8 convolution_convert_fusion
  536.2 0.2 reduce-scatter.15.cloned.1.call-start
  536.4 16.6 %all-gather.10.cloned.1.call-done = bf16[512,1024]{1,0:T(8,128)(2,1)} async-done(((bf16[128,1024]{1,0:T(8,128)(2,1)}), bf16[512,1024]{1,0:T(8,128)(2,1)}) %all-gather.10.cloned.1.call-update) | async-done | bytes 1048592 | tf_op jit(solution)/shard_map/all_gather | solution.py:74
  553.0 10.3 %fusion.12 = f32[3584,512]{1,0:T(8,128)} fusion(bf16[3584,1024]{1,0:T(8,128)(2,1)} %mul.106, bf16[512,1024]{1,0:T(8,128)(2,1)} %all-gather.10.cloned.1.call-done), kind=kOutput, calls=%fused_computation.29 | convolution fusion | flops 3758096384 | bytes 15728640
  563.3 133.0 %reduce-scatter.15.cloned.1.call-done = f32[448,512]{1,0:T(8,128)} async-done(((f32[3584,512]{1,0:T(8,128)}), f32[448,512]{1,0:T(8,128)}) %reduce-scatter.15.cloned.1.call-update) | async-done | bytes 917520 | tf_op jit(solution)/shard_map/reduce_scatter | solution.py:75
  696.3 2.6 multiply_convert_fusion.1
  699.0 0.7 all-gather.14.cloned.1.call-update
  699.7 64.6 %all-gather.12.cloned.1.call-done = bf16[3584,512]{1,0:T(8,128)(2,1)} async-done(((bf16[448,512]{1,0:T(8,128)(2,1)}), bf16[3584,512]{1,0:T(8,128)(2,1)}) %all-gather.12.cloned.1.call-update) | async-done | bytes 3670032 | tf_op jit(solution)/shard_map/all_gather | solution.py:88
  764.4 9.5 fusion.13
  773.9 57.6 %all-gather.14.cloned.1.call-done = bf16[3584,512]{1,0:T(8,128)(2,1)} async-done(((bf16[448,512]{1,0:T(8,128)(2,1)}), bf16[3584,512]{1,0:T(8,128)(2,1)}) %all-gather.14.cloned.1.call-update) | async-done | bytes 3670032 | tf_op jit(solution)/shard_map/all_gather | solution.py:89
  831.5 10.1 convolution_add_fusion
  841.9 12.7 %mul.115 = f32[16,64,56,64]{1,0,3,2:T(8,128)} broadcast(f32[16,56]{0,1:T(8,128)S(1)} %copy.37), dimensions={0,2} | broadcast | bytes 14683648 | tf_op jit(solution)/shard_map/mul | solution.py:17
  854.6 25.2 %mul.116 = f32[1024,3584]{0,1:T(8,128)} reshape(f32[16,64,56,64]{1,0,3,2:T(8,128)} %mul.115) | data formatting | bytes 29360128 | tf_op jit(solution)/shard_map/mul | solution.py:17
  879.8 11.6 %mul.118 = f32[16,64,56,64]{1,0,3,2:T(8,128)} broadcast(f32[16,56]{0,1:T(8,128)S(1)} %copy.38), dimensions={0,2} | broadcast | bytes 14683648 | tf_op jit(solution)/shard_map/mul | solution.py:17
  891.4 24.9 %mul.119 = f32[1024,3584]{0,1:T(8,128)} reshape(f32[16,64,56,64]{1,0,3,2:T(8,128)} %mul.118) | data formatting | bytes 29360128 | tf_op jit(solution)/shard_map/mul | solution.py:17
  916.3 11.6 %mul.121 = f32[56,64,16,64]{3,2,1,0:T(8,128)} broadcast(f32[56,16]{1,0:T(8,128)S(1)} %copy.39), dimensions={0,2} | broadcast | bytes 14683648 | tf_op jit(solution)/shard_map/mul | solution.py:17
  928.0 25.0 %mul.122 = f32[3584,1024]{1,0:T(8,128)} reshape(f32[56,64,16,64]{3,2,1,0:T(8,128)} %mul.121) | data formatting | bytes 29360128 | tf_op jit(solution)/shard_map/mul | solution.py:17
  953.0 0.5 log_subtract_fusion
  953.5 10.3 %multiply_convert_fusion = bf16[3584,1024]{1,0:T(8,128)(2,1)} fusion(f32[3584,1024]{1,0:T(8,128)} %mul.122, bf16[3584,512]{1,0:T(8,128)(2,1)} %all-gather.8.cloned.1.call-done, bf16[512,1024]{1,0:T(8,128)(2,1)S(1)} %copy-done.8), kind=kOutput, calls=%fused_computation.5 | convolution fusion | flops 3765436416 | bytes 26738688 | tf_op jit(solution)/shard_map/dot_general | solution.py:93
  963.8 9.1 fusion.1
  972.9 9.9 copy.40
  982.8 10.2 %fusion = bf16[1024,3584]{0,1:T(8,128)(2,1)} fusion(f32[1024,3584]{0,1:T(8,128)} %mul.119, bf16[3584,512]{1,0:T(8,128)(2,1)} %all-gather.14.cloned.1.call-done, bf16[512,1024]{1,0:T(8,128)(2,1)S(1)} %copy-done.5), kind=kOutput, calls=%fused_computation.2 | convolution fusion | flops 3765436416 | bytes 26738688 | tf_op jit(solution)/shard_map/dot_general | solution.py:111
  993.0 10.0 copy.41
  1003.0 1.8 add_convert_fusion
  (48 shorter events, 0.8 us)
Async XLA Ops:
  7.2 453.0 %copy-start = (bf16[1024,128]{1,0:T(8,128)(2,1)S(1)}, bf16[1024,128]{1,0:T(8,128)(2,1)}, u32[]{:S(2)}) copy-start(bf16[1024,128]{1,0:T(8,128)(2,1)} %param.16) | copy-start | bytes 786436
  7.2 74.0 %all-gather.6.cloned.1.call-start = ((), (), s32[]{:S(2)}) async-start(), calls=%async_computation.4 | async-start | bytes 1310720 | tf_op jit(solution)/shard_map/all_gather | solution.py:46
  7.9 344.7 %reduce-scatter.13.cloned.1.call-start = ((), (), s32[]{:S(2)}) async-start(), calls=%async_computation.12 | async-start | bytes 16515072 | tf_op jit(solution)/shard_map/reduce_scatter | solution.py:53
  15.9 18.9 %copy-start.9 = (s32[16,56]{1,0:T(8,128)S(1)}, s32[16,56]{1,0:T(8,128)}, u32[]{:S(2)}) copy-start(s32[16,56]{1,0:T(8,128)} %param.13) | copy-start | bytes 10756
  81.2 6.7 copy-start.4
  81.2 6.7 copy-start.5
  113.0 242.2 %copy-start.10 = (s32[56,16]{0,1:T(8,128)S(1)}, s32[56,16]{0,1:T(8,128)}, u32[]{:S(2)}) copy-start(s32[56,16]{0,1:T(8,128)} %param.15) | copy-start | bytes 10756
  113.0 307.6 %all-gather.8.cloned.1.call-start = ((), (), s32[]{:S(2)}) async-start(), calls=%async_computation.5 | async-start | bytes 4128768 | tf_op jit(solution)/shard_map/all_gather | solution.py:62
  355.1 105.0 %reduce-scatter.9.cloned.1.call-start = ((), (), s32[]{:S(2)}) async-start(), calls=%async_computation.6 | async-start | bytes 2621440 | tf_op jit(solution)/shard_map/reduce_scatter | solution.py:63
  395.1 65.1 %copy-start.7 = (bf16[128,1024]{1,0:T(8,128)(2,1)S(1)}, bf16[128,1024]{1,0:T(8,128)(2,1)}, u32[]{:S(2)}) copy-start(bf16[128,1024]{1,0:T(8,128)(2,1)} %param.9) | copy-start | bytes 786436
  395.1 138.2 %copy-start.11 = (s32[128]{0:T(128)S(1)}, s32[128]{0:T(128)}, u32[]{:S(2)}) copy-start(s32[128]{0:T(128)} %param.17) | copy-start | bytes 1540
  430.1 103.2 %all-reduce.2.cloned.1.call-start = ((), (), s32[]{:S(2)}) async-start(), calls=%async_computation.7 | async-start | bytes 131072 | tf_op jit(solution)/shard_map/psum | solution.py:68
  462.1 90.9 %all-gather.10.cloned.1.call-start = ((), (), s32[]{:S(2)}) async-start(), calls=%async_computation.8 | async-start | bytes 1310720 | tf_op jit(solution)/shard_map/all_gather | solution.py:74
  536.2 160.1 %reduce-scatter.15.cloned.1.call-start = ((), (), s32[]{:S(2)}) async-start(), calls=%async_computation.13 | async-start | bytes 8257536 | tf_op jit(solution)/shard_map/reduce_scatter | solution.py:75
  563.2 133.1 %copy-start.3 = (f32[448,1024]{1,0:T(8,128)S(1)}, f32[448,1024]{1,0:T(8,128)}, u32[]{:S(2)}) copy-start(f32[448,1024]{1,0:T(8,128)} %reduce-scatter.13.cloned.1.call-done) | copy-start | bytes 5505028
  563.3 201.1 %all-gather.12.cloned.1.call-start = ((), (), s32[]{:S(2)}) async-start(), calls=%async_computation.9 | async-start | bytes 4128768 | tf_op jit(solution)/shard_map/all_gather | solution.py:88
  699.0 132.6 %all-gather.14.cloned.1.call-start = ((), (), s32[]{:S(2)}) async-start(), calls=%async_computation.10 | async-start | bytes 4128768 | tf_op jit(solution)/shard_map/all_gather | solution.py:89
  699.7 303.3 %reduce-scatter.11.cloned.1.call-start = ((), (), s32[]{:S(2)}) async-start(), calls=%async_computation.11 | async-start | bytes 2621440 | tf_op jit(solution)/shard_map/reduce_scatter | solution.py:121
  928.0 25.5 %copy-start.8 = (bf16[512,1024]{1,0:T(8,128)(2,1)S(1)}, bf16[512,1024]{1,0:T(8,128)(2,1)}, u32[]{:S(2)}) copy-start(bf16[512,1024]{1,0:T(8,128)(2,1)} %all-gather.10.cloned.1.call-done) | copy-start | bytes 3145732
  953.5 10.3 %copy-start.2 = (bf16[3584,512]{1,0:T(8,128)(2,1)S(1)}, bf16[3584,512]{1,0:T(8,128)(2,1)}, u32[]{:S(2)}) copy-start(bf16[3584,512]{1,0:T(8,128)(2,1)} %all-gather.12.cloned.1.call-done) | copy-start | bytes 11010052
  982.8 22.0 %copy-start.1 = (bf16[1024,128]{1,0:T(8,128)(2,1)S(1)}, bf16[1024,128]{1,0:T(8,128)(2,1)}, u32[]{:S(2)}) copy-start(bf16[1024,128]{1,0:T(8,128)(2,1)} %param.16) | copy-start | bytes 786436
  993.0 10.0 copy-start.6
Sparse Core Ops, SparseCore 0:
  9.5 19.4 all-gather.5
  113.2 239.4 reduce-scatter.12
  355.3 65.2 all-gather.7
  430.2 29.8 reduce-scatter.8
  464.0 69.2 all-reduce.1
  536.3 16.6 all-gather.9
  563.4 132.8 reduce-scatter.14
  699.1 65.2 all-gather.11
  766.6 64.9 all-gather.13
  841.8 29.8 reduce-scatter.10
where the time goes:
time: 1020 us; the launch traced here: 1010 us
  waiting for transfers between devices  640 us (63%)
  local copies, waits for them, and re-layouts  226 us (22%)
  matrix products  83.3 us (8%)
  other arithmetic  47.7 us (5%)
  between operations  14.5 us (1%)
    reduce_scatter x1, waiting for transfers between devices, shards(): lax.psum_scatter(jnp.concatenate([gate_part, up_part], axis=1), 'row', sc...  240 us
    mul x12, local copies, waits for them, and re-layouts, masked(): pruned = blocks * block_mask[:, None, :, None].astype(weight.dtype)  190 us
    reduce_scatter x1, waiting for transfers between devices, shards(): lax.psum_scatter(lax.dot_general(down_kept, dmixed_all, (((1,), (1,)), ((...  133 us
    psum x1, waiting for transfers between devices, shards(): logits = lax.psum(partial_value, 'row')  71.2 us
    all_gather x1, waiting for transfers between devices, shards(): lax.all_gather(gate_delta, 'row', axis=0, tiled=True)  64.6 us
    all_gather x1, waiting for transfers between devices, shards(): lax.all_gather(up_delta, 'row', axis=0, tiled=True)  57.6 us
    unnamed x27, local copies, waits for them, and re-layouts  35.6 us
    mul x3, other arithmetic, masked(): pruned = blocks * block_mask[:, None, :, None].astype(weight.dtype)  32.9 us
  transfers between devices with their start and end apart: 10, of which 8 were waited for; matrix products, arithmetic and copies ran while one was open for 28% of the time, Pallas kernels for 0%

commit v1 on v0

--- a/solution.py
+++ b/solution.py
@@ -65,7 +65,7 @@
     )
     mixed_rows = (tokens.astype(jnp.float32) + branch).astype(jnp.bfloat16)
     partial_value = jnp.dot(mixed_rows, head_weight, preferred_element_type=jnp.float32)
-    logits = lax.psum(partial_value, "row")
+    logits = jnp.sum(lax.all_gather(partial_value, "row"), axis=0)
     token_loss, grad_full = classify(logits, labels)
     dlogits = grad_full.astype(jnp.bfloat16)
     dmixed = lax.dot_general(

time: 1020 us -> 976 us (0.957)
  waiting for transfers between devices: 640 us -> 568 us
  blocking collectives: 0 us -> 31.5 us
    psum x1 -> x0, waiting for transfers between devices: 71.2 us -> none  [shards(): logits = lax.psum(partial_value, 'row')]
    all_gather x0 -> x1, blocking collectives: none -> 31.5 us  [shards(): logits = jnp.sum(lax.all_gather(partial_value, 'row'), axis=0)]
  transfers between devices with their start and end apart: 10 -> 9, of which waited for: 8 -> 7; matrix products, arithmetic and copies ran while one was open for 28% -> 29% of each run, Pallas kernels for 0% -> 0%
where the time goes in v1:
time: 976 us; the launch traced here: 970 us
  waiting for transfers between devices  568 us (58%)
  local copies, waits for them, and re-layouts  226 us (23%)
  matrix products  81.9 us (8%)
  other arithmetic  46.8 us (5%)
  blocking collectives  31.5 us (3%)
  between operations  14.2 us (1%)
    reduce_scatter x1, waiting for transfers between devices, shards(): lax.psum_scatter(jnp.concatenate([gate_part, up_part], axis=1), 'row', sc...  240 us
    mul x12, local copies, waits for them, and re-layouts, masked(): pruned = blocks * block_mask[:, None, :, None].astype(weight.dtype)  190 us
    reduce_scatter x1, waiting for transfers between devices, shards(): lax.psum_scatter(lax.dot_general(down_kept, dmixed_all, (((1,), (1,)), ((...  133 us
    all_gather x1, waiting for transfers between devices, shards(): lax.all_gather(gate_delta, 'row', axis=0, tiled=True)  64.6 us
    all_gather x1, waiting for transfers between devices, shards(): lax.all_gather(up_delta, 'row', axis=0, tiled=True)  57.6 us
    unnamed x27, local copies, waits for them, and re-layouts  35.7 us
    mul x3, other arithmetic, masked(): pruned = blocks * block_mask[:, None, :, None].astype(weight.dtype)  32.9 us
    all_gather x1, blocking collectives, shards(): logits = jnp.sum(lax.all_gather(partial_value, 'row'), axis=0)  31.5 us
  transfers between devices with their start and end apart: 9, of which 7 were waited for; matrix products, arithmetic and copies ran while one was open for 29% of the time, Pallas kernels for 0%

profile of v1, /device:TPU:0, one launch (start us, length us, event | category | flops | bytes accessed | tf_op | source)
XLA Modules:
  0.0 969.6 jit_solution(13632425199118753057)
XLA Ops:
  7.2 0.7 all-gather.7.cloned.1.call-update
  8.0 0.8 fusion.9
  8.7 7.2 mul.99
  15.9 18.9 %mul.100 = bf16[1024,3584]{1,0:T(8,128)(2,1)} reshape(bf16[16,64,56,64]{3,2,1,0:T(8,128)(2,1)} %mul.99) | data formatting | bytes 14680064 | tf_op jit(solution)/shard_map/mul | solution.py:17
  34.9 7.2 mul.96
  42.1 18.7 %mul.97 = bf16[1024,3584]{1,0:T(8,128)(2,1)} reshape(bf16[16,64,56,64]{3,2,1,0:T(8,128)(2,1)} %mul.96) | data formatting | bytes 14680064 | tf_op jit(solution)/shard_map/mul | solution.py:17
  60.8 10.2 %mul.101 = bf16[1024,3584]{1,0:T(8,128)(2,1)} multiply(bf16[1024,3584]{1,0:T(8,128)(2,1)} %param.11, bf16[1024,3584]{1,0:T(8,128)(2,1)} %mul.100) | non-fusion elementwise | flops 3670016 | bytes 22020096 | tf_op jit(solution)/shard_map/mul | solution.py:17
  71.0 10.2 %mul.98 = bf16[1024,3584]{1,0:T(8,128)(2,1)} multiply(bf16[1024,3584]{1,0:T(8,128)(2,1)} %param.10, bf16[1024,3584]{1,0:T(8,128)(2,1)} %mul.97) | non-fusion elementwise | flops 3670016 | bytes 22020096 | tf_op jit(solution)/shard_map/mul | solution.py:17
  81.2 6.6 fusion.15
  87.9 4.0 fusion.14
  91.8 5.4 pad_maximum_fusion
  97.3 15.7 %copy.53 = f32[3584,1024]{1,0:T(8,128)} copy(f32[3584,1024]{0,1:T(8,128)} %pad_maximum_fusion) | data formatting | bytes 29360128
  113.0 239.5 %reduce-scatter.13.cloned.1.call-done = f32[448,1024]{1,0:T(8,128)} async-done(((f32[3584,1024]{1,0:T(8,128)}), f32[448,1024]{1,0:T(8,128)}) %reduce-scatter.13.cloned.1.call-update) | async-done | bytes 1835024 | tf_op jit(solution)/shard_map/reduce_scatter | solution.py:53
  352.6 2.5 multiply_convert_fusion.3
  355.1 0.1 copy.43
  355.2 7.2 mul.104
  362.4 20.1 %mul.105 = bf16[3584,1024]{1,0:T(8,128)(2,1)} reshape(bf16[56,64,16,64]{3,2,1,0:T(8,128)(2,1)} %mul.104) | data formatting | bytes 14680064 | tf_op jit(solution)/shard_map/mul | solution.py:17
  382.5 12.5 %mul.106 = bf16[3584,1024]{1,0:T(8,128)(2,1)} multiply(bf16[3584,1024]{1,0:T(8,128)(2,1)} %param.12, bf16[3584,1024]{1,0:T(8,128)(2,1)} %mul.105) | non-fusion elementwise | flops 3670016 | bytes 22020096 | tf_op jit(solution)/shard_map/mul | solution.py:17
  395.0 25.5 %all-gather.9.cloned.1.call-done = bf16[3584,512]{1,0:T(8,128)(2,1)} async-done(((bf16[448,512]{1,0:T(8,128)(2,1)}), bf16[3584,512]{1,0:T(8,128)(2,1)}) %all-gather.9.cloned.1.call-update) | async-done | bytes 3670032 | tf_op jit(solution)/shard_map/all_gather | solution.py:62
  420.5 9.5 fusion.11
  430.1 30.0 %reduce-scatter.9.cloned.1.call-done = f32[128,1024]{1,0:T(8,128)} async-done(((f32[512,1024]{1,0:T(8,128)}), f32[128,1024]{1,0:T(8,128)}) %reduce-scatter.9.cloned.1.call-update) | async-done | bytes 524304 | tf_op jit(solution)/shard_map/reduce_scatter | solution.py:63
  460.1 1.3 fusion.3
  461.4 31.5 %all-gather = f32[1024,128]{1,0:T(8,128)S(1)} all-gather(f32[128,128]{1,0:T(8,128)S(1)} %fusion.3), channel_id=2, replica_groups=mesh['row'=8,'col'=4] {'row'}, dimensions={0}, use_global_device_ids=true | all-gather | bytes 589824 | tf_op jit(solution)/shard_map/all_gather | solution.py:68
  492.9 0.2 exponential_reduce_fusion
  493.1 1.0 convolution_convert_fusion
  494.1 0.2 reduce-scatter.15.cloned.1.call-start
  494.3 16.7 %all-gather.11.cloned.1.call-done = bf16[512,1024]{1,0:T(8,128)(2,1)} async-done(((bf16[128,1024]{1,0:T(8,128)(2,1)}), bf16[512,1024]{1,0:T(8,128)(2,1)}) %all-gather.11.cloned.1.call-update) | async-done | bytes 1048592 | tf_op jit(solution)/shard_map/all_gather | solution.py:74
  511.0 10.3 %fusion.12 = f32[3584,512]{1,0:T(8,128)} fusion(bf16[3584,1024]{1,0:T(8,128)(2,1)} %mul.106, bf16[512,1024]{1,0:T(8,128)(2,1)} %all-gather.11.cloned.1.call-done), kind=kOutput, calls=%fused_computation.29 | convolution fusion | flops 3758096384 | bytes 15728640
  521.3 133.0 %reduce-scatter.15.cloned.1.call-done = f32[448,512]{1,0:T(8,128)} async-done(((f32[3584,512]{1,0:T(8,128)}), f32[448,512]{1,0:T(8,128)}) %reduce-scatter.15.cloned.1.call-update) | async-done | bytes 917520 | tf_op jit(solution)/shard_map/reduce_scatter | solution.py:75
  654.3 2.6 multiply_convert_fusion.1
  657.0 0.7 all-gather.15.cloned.1.call-update
  657.8 64.6 %all-gather.13.cloned.1.call-done = bf16[3584,512]{1,0:T(8,128)(2,1)} async-done(((bf16[448,512]{1,0:T(8,128)(2,1)}), bf16[3584,512]{1,0:T(8,128)(2,1)}) %all-gather.13.cloned.1.call-update) | async-done | bytes 3670032 | tf_op jit(solution)/shard_map/all_gather | solution.py:88
  722.4 9.5 fusion.13
  731.9 57.6 %all-gather.15.cloned.1.call-done = bf16[3584,512]{1,0:T(8,128)(2,1)} async-done(((bf16[448,512]{1,0:T(8,128)(2,1)}), bf16[3584,512]{1,0:T(8,128)(2,1)}) %all-gather.15.cloned.1.call-update) | async-done | bytes 3670032 | tf_op jit(solution)/shard_map/all_gather | solution.py:89
  789.5 10.1 %convolution_add_fusion = f32[512,1024]{1,0:T(8,128)} fusion(f32[512,1024]{1,0:T(8,128)} %fusion.13, bf16[3584,512]{1,0:T(8,128)(2,1)} %all-gather.15.cloned.1.call-done, bf16[1024,3584]{1,0:T(8,128)(2,1)} %mul.101), kind=kOutput, calls=%fused_computation.6 | convolution fusion | flops 3758620672 | bytes 15204352 | tf_op jit(solution)/shard_map/dot_general | solution.py:32
  799.9 12.7 %mul.115 = f32[16,64,56,64]{1,0,3,2:T(8,128)} broadcast(f32[16,56]{0,1:T(8,128)S(1)} %copy.47), dimensions={0,2} | broadcast | bytes 14683648 | tf_op jit(solution)/shard_map/mul | solution.py:17
  812.6 25.2 %mul.116 = f32[1024,3584]{0,1:T(8,128)} reshape(f32[16,64,56,64]{1,0,3,2:T(8,128)} %mul.115) | data formatting | bytes 29360128 | tf_op jit(solution)/shard_map/mul | solution.py:17
  837.8 11.6 %mul.118 = f32[16,64,56,64]{1,0,3,2:T(8,128)} broadcast(f32[16,56]{0,1:T(8,128)S(1)} %copy.48), dimensions={0,2} | broadcast | bytes 14683648 | tf_op jit(solution)/shard_map/mul | solution.py:17
  849.4 24.9 %mul.119 = f32[1024,3584]{0,1:T(8,128)} reshape(f32[16,64,56,64]{1,0,3,2:T(8,128)} %mul.118) | data formatting | bytes 29360128 | tf_op jit(solution)/shard_map/mul | solution.py:17
  874.4 11.6 %mul.121 = f32[56,64,16,64]{3,2,1,0:T(8,128)} broadcast(f32[56,16]{1,0:T(8,128)S(1)} %copy.49), dimensions={0,2} | broadcast | bytes 14683648 | tf_op jit(solution)/shard_map/mul | solution.py:17
  886.0 25.0 %mul.122 = f32[3584,1024]{1,0:T(8,128)} reshape(f32[56,64,16,64]{3,2,1,0:T(8,128)} %mul.121) | data formatting | bytes 29360128 | tf_op jit(solution)/shard_map/mul | solution.py:17
  911.0 0.5 log_subtract_fusion
  911.5 10.3 %multiply_convert_fusion = bf16[3584,1024]{1,0:T(8,128)(2,1)} fusion(f32[3584,1024]{1,0:T(8,128)} %mul.122, bf16[3584,512]{1,0:T(8,128)(2,1)} %all-gather.9.cloned.1.call-done, bf16[512,1024]{1,0:T(8,128)(2,1)S(1)} %copy-done.8), kind=kOutput, calls=%fused_computation.5 | convolution fusion | flops 3765436416 | bytes 26738688 | tf_op jit(solution)/shard_map/dot_general | solution.py:93
  921.8 9.1 fusion.1
  930.9 9.9 %copy.50 = bf16[1024,3584]{1,0:T(8,128)(2,1)} copy(bf16[1024,3584]{0,1:T(8,128)(2,1)} %fusion.1) | data formatting | bytes 14680064
  940.8 10.3 %fusion = bf16[1024,3584]{0,1:T(8,128)(2,1)} fusion(f32[1024,3584]{0,1:T(8,128)} %mul.119, bf16[3584,512]{1,0:T(8,128)(2,1)} %all-gather.15.cloned.1.call-done, bf16[512,1024]{1,0:T(8,128)(2,1)S(1)} %copy-done.5), kind=kOutput, calls=%fused_computation.2 | convolution fusion | flops 3765436416 | bytes 26738688 | tf_op jit(solution)/shard_map/dot_general | solution.py:111
  951.1 10.0 %copy.51 = bf16[1024,3584]{1,0:T(8,128)(2,1)} copy(bf16[1024,3584]{0,1:T(8,128)(2,1)} %fusion) | data formatting | bytes 14680064
  961.0 1.8 add_convert_fusion
  (47 shorter events, 0.8 us)
Async XLA Ops:
  7.2 452.9 %copy-start = (bf16[1024,128]{1,0:T(8,128)(2,1)S(1)}, bf16[1024,128]{1,0:T(8,128)(2,1)}, u32[]{:S(2)}) copy-start(bf16[1024,128]{1,0:T(8,128)(2,1)} %param.16) | copy-start | bytes 786436
  7.2 74.0 %all-gather.7.cloned.1.call-start = ((), (), s32[]{:S(2)}) async-start(), calls=%async_computation.4 | async-start | bytes 1310720 | tf_op jit(solution)/shard_map/all_gather | solution.py:46
  7.9 344.6 %reduce-scatter.13.cloned.1.call-start = ((), (), s32[]{:S(2)}) async-start(), calls=%async_computation.11 | async-start | bytes 16515072 | tf_op jit(solution)/shard_map/reduce_scatter | solution.py:53
  15.9 18.9 %copy-start.9 = (s32[16,56]{1,0:T(8,128)S(1)}, s32[16,56]{1,0:T(8,128)}, u32[]{:S(2)}) copy-start(s32[16,56]{1,0:T(8,128)} %param.13) | copy-start | bytes 10756
  81.2 6.7 copy-start.4
  81.2 6.7 copy-start.5
  113.0 242.1 %copy-start.10 = (s32[56,16]{0,1:T(8,128)S(1)}, s32[56,16]{0,1:T(8,128)}, u32[]{:S(2)}) copy-start(s32[56,16]{0,1:T(8,128)} %param.15) | copy-start | bytes 10756
  113.0 307.5 %all-gather.9.cloned.1.call-start = ((), (), s32[]{:S(2)}) async-start(), calls=%async_computation.5 | async-start | bytes 4128768 | tf_op jit(solution)/shard_map/all_gather | solution.py:62
  355.1 105.0 %reduce-scatter.9.cloned.1.call-start = ((), (), s32[]{:S(2)}) async-start(), calls=%async_computation.6 | async-start | bytes 2621440 | tf_op jit(solution)/shard_map/reduce_scatter | solution.py:63
  395.0 65.1 %copy-start.7 = (bf16[128,1024]{1,0:T(8,128)(2,1)S(1)}, bf16[128,1024]{1,0:T(8,128)(2,1)}, u32[]{:S(2)}) copy-start(bf16[128,1024]{1,0:T(8,128)(2,1)} %param.9) | copy-start | bytes 786436
  395.0 97.9 %copy-start.11 = (s32[128]{0:T(128)S(1)}, s32[128]{0:T(128)}, u32[]{:S(2)}) copy-start(s32[128]{0:T(128)} %param.17) | copy-start | bytes 1540
  430.0 81.0 %all-gather.11.cloned.1.call-start = ((), (), s32[]{:S(2)}) async-start(), calls=%async_computation.7 | async-start | bytes 1310720 | tf_op jit(solution)/shard_map/all_gather | solution.py:74
  494.1 160.2 %reduce-scatter.15.cloned.1.call-start = ((), (), s32[]{:S(2)}) async-start(), calls=%async_computation.12 | async-start | bytes 8257536 | tf_op jit(solution)/shard_map/reduce_scatter | solution.py:75
  521.3 133.1 %copy-start.3 = (f32[448,1024]{1,0:T(8,128)S(1)}, f32[448,1024]{1,0:T(8,128)}, u32[]{:S(2)}) copy-start(f32[448,1024]{1,0:T(8,128)} %reduce-scatter.13.cloned.1.call-done) | copy-start | bytes 5505028
  521.3 201.1 %all-gather.13.cloned.1.call-start = ((), (), s32[]{:S(2)}) async-start(), calls=%async_computation.8 | async-start | bytes 4128768 | tf_op jit(solution)/shard_map/all_gather | solution.py:88
  657.0 132.6 %all-gather.15.cloned.1.call-start = ((), (), s32[]{:S(2)}) async-start(), calls=%async_computation.9 | async-start | bytes 4128768 | tf_op jit(solution)/shard_map/all_gather | solution.py:89
  657.7 303.3 %reduce-scatter.11.cloned.1.call-start = ((), (), s32[]{:S(2)}) async-start(), calls=%async_computation.10 | async-start | bytes 2621440 | tf_op jit(solution)/shard_map/reduce_scatter | solution.py:121
  886.0 25.5 %copy-start.8 = (bf16[512,1024]{1,0:T(8,128)(2,1)S(1)}, bf16[512,1024]{1,0:T(8,128)(2,1)}, u32[]{:S(2)}) copy-start(bf16[512,1024]{1,0:T(8,128)(2,1)} %all-gather.11.cloned.1.call-done) | copy-start | bytes 3145732
  911.5 10.3 %copy-start.2 = (bf16[3584,512]{1,0:T(8,128)(2,1)S(1)}, bf16[3584,512]{1,0:T(8,128)(2,1)}, u32[]{:S(2)}) copy-start(bf16[3584,512]{1,0:T(8,128)(2,1)} %all-gather.13.cloned.1.call-done) | copy-start | bytes 11010052
  940.8 22.0 %copy-start.1 = (bf16[1024,128]{1,0:T(8,128)(2,1)S(1)}, bf16[1024,128]{1,0:T(8,128)(2,1)}, u32[]{:S(2)}) copy-start(bf16[1024,128]{1,0:T(8,128)(2,1)} %param.16) | copy-start | bytes 786436
  951.1 10.0 %copy-start.6 = (bf16[128,1024]{1,0:T(8,128)(2,1)S(1)}, bf16[128,1024]{1,0:T(8,128)(2,1)}, u32[]{:S(2)}) copy-start(bf16[128,1024]{1,0:T(8,128)(2,1)} %convolution_convert_fusion) | copy-start | bytes 786436
Sparse Core Ops, SparseCore 0:
  9.5 19.4 all-gather.6
  113.1 239.3 reduce-scatter.12
  355.2 65.2 all-gather.8
  430.2 29.8 reduce-scatter.8
  494.2 16.7 all-gather.10
  521.4 132.8 reduce-scatter.14
  657.1 65.2 all-gather.12
  724.6 64.9 all-gather.14
  799.8 29.8 reduce-scatter.10
